TPU v7x, 32 devices: a whole 2x2x4 slice. The times are simulated.
32 devices in a mesh: dp: 2 (over x), row: 4 (over z), col: 4 (over y, core).
Axes of the slice: x: 2, y: 2, z: 4, core: 2. Of those that a mesh axis runs over, the one named last changes fastest.
Arguments:
- tokens: bfloat16 [2, 768, 4096], P(None, 'row', ('dp', 'col')), may hold values from -6 to 6
- w_query: bfloat16 [768, 768], P(('row', 'dp'), 'col'), may hold values from -0.21875 to 0.21875
- w_key: bfloat16 [768, 768], P(('row', 'dp'), 'col'), may hold values from -0.21875 to 0.21875
- w_value: bfloat16 [768, 768], P(('row', 'dp'), 'col'), may hold values from -0.21875 to 0.21875
- w_output: bfloat16 [768, 768], P(('col', 'dp'), 'row'), may hold values from -6 to 6
- w_inner: bfloat16 [768, 3072], P(('row', 'dp'), 'col'), may hold values from -0.21875 to 0.21875
- w_outer: bfloat16 [3072, 768], P(('col', 'dp'), 'row'), may hold values from -0.109375 to 0.109375
- first_gain: float32 [768], P('row'), may hold values from 0.1 to 1.9
- first_shift: float32 [768], P('row'), may hold values from -3 to 3
- second_gain: float32 [768], P('row'), may hold values from 0.1 to 1.9
- second_shift: float32 [768], P('row'), may hold values from -3 to 3
- seq_lengths: int32 [2, 2], replicated, may hold values from 512 to 2048, as said below
- out_grad: bfloat16 [2, 768, 4096], P(None, 'row', ('dp', 'col')), may hold values from -6 to 6
Outputs:
- mixed: bfloat16 [2, 768, 4096], P(None, 'row', ('dp', 'col'))
- d_input: float32 [2, 768, 4096], P(None, 'row', ('dp', 'col'))
- grad_w_query: float32 [768, 768], P(('row', 'dp'), 'col')
- grad_w_key: float32 [768, 768], P(('row', 'dp'), 'col')
- grad_w_value: float32 [768, 768], P(('row', 'dp'), 'col')
- grad_w_output: float32 [768, 768], P(('col', 'dp'), 'row')
- grad_w_inner: float32 [768, 3072], P(('row', 'dp'), 'col')
- grad_w_outer: float32 [3072, 768], P(('col', 'dp'), 'row')
- grad_first_gain: float32 [768], P('row')
- grad_first_shift: float32 [768], P('row')
- grad_second_gain: float32 [768], P('row')
- grad_second_shift: float32 [768], P('row')
Inputs may be any that keep to these rules, and one draw needn't show every extreme that they name: micro-batch m's sequence in data group g fills the first seq_lengths[m, g] positions of the group's slot of 2048 token slots; in every draw some sequence has exactly 2048 tokens and some exactly 512.
All inputs are finite; a program needn't handle non-finite values.
Results may differ from a plain program's by a relative error of at most 0.02.
Values may be sent and summed in bfloat16 or wider, within the bound.
No kernel may reach another device: no remote copies, remote signals or barrier semaphores. Data moves between devices by JAX's collectives and lax.ppermute only.
A program may use at most 128 MiB of HBM per device.

v0:
```python
import jax
import jax.numpy as jnp
from jax import lax
from jax.sharding import PartitionSpec as P

HD = 64
norm_eps = 1e-05
masked_score = -1e30


def rotate_pairs(values, positions, head_size, direction):
    row_count = values.shape[0]
    row_width = values.shape[1]
    half_size = head_size // 2
    frequency = 10000.0 ** (-2.0 * jnp.arange(half_size, dtype=jnp.float32) / head_size)
    angles = positions.astype(jnp.float32)[:, None] * frequency[None, :]
    cosine = jnp.cos(angles)[:, None, :]
    sine_part = direction * jnp.sin(angles)[:, None, :]
    paired = values.reshape(row_count, row_width // head_size, half_size, 2)
    even_part = paired[..., 0]
    odd_part = paired[..., 1]
    turned = jnp.stack(
        [even_part * cosine - odd_part * sine_part, even_part * sine_part + odd_part * cosine],
        axis=-1,
    )
    return turned.reshape(row_count, row_width)


def fetch_blocks(w_query, w_key, w_value, w_output, w_inner, w_outer):
    return (
        lax.all_gather(w_query, "dp", axis=0, tiled=True),
        lax.all_gather(w_key, "dp", axis=0, tiled=True),
        lax.all_gather(w_value, "dp", axis=0, tiled=True),
        lax.all_gather(w_output, "dp", axis=0, tiled=True),
        lax.all_gather(w_inner, "dp", axis=0, tiled=True),
        lax.all_gather(w_outer, "dp", axis=0, tiled=True),
    )


def along_col(values):
    return lax.all_gather(values, "col", axis=0, tiled=True)


def along_row(values):
    return lax.all_gather(values, "row", axis=0, tiled=True)


def reduce_rows(values):
    return lax.psum_scatter(values, "row", scatter_dimension=0, tiled=True)


def reduce_cols(values):
    return lax.psum_scatter(
        values.astype(jnp.bfloat16), "col", scatter_dimension=0, tiled=True
    ).astype(jnp.float32)


def feature_totals(first_sum, second_sum):
    return lax.psum((first_sum, second_sum), "row")


def contract_rows(left, right):
    return lax.dot_general(
        left, right, (((0,), (0,)), ((), ())), preferred_element_type=jnp.float32
    )


def times_transpose(left, right):
    return lax.dot_general(
        left, right, (((1,), (1,)), ((), ())), preferred_element_type=jnp.float32
    )


def layer_norm(summed, gain_vec, shift_vec, full_width):
    first_sum, second_sum = feature_totals(
        jnp.sum(summed, axis=1), jnp.sum(summed * summed, axis=1)
    )
    row_mean = first_sum / full_width
    row_var = second_sum / full_width - row_mean * row_mean
    inv_scale = lax.rsqrt(row_var + norm_eps)
    centered = (summed - row_mean[:, None]) * inv_scale[:, None]
    return (centered * gain_vec + shift_vec, centered, inv_scale)


def layer_norm_back(grad_out, centered, inv_scale, gain_vec, full_width):
    grad_cent = grad_out * gain_vec
    first_sum, second_sum = feature_totals(
        jnp.sum(grad_cent, axis=1), jnp.sum(grad_cent * centered, axis=1)
    )
    return inv_scale[:, None] * (
        grad_cent - first_sum[:, None] / full_width - centered * (second_sum / full_width)[:, None]
    )


def split_heads(values, head_size):
    row_count = values.shape[0]
    return values.reshape(row_count, values.shape[1] // head_size, head_size).transpose(1, 0, 2)


def merge_heads(values):
    return values.transpose(1, 0, 2).reshape(values.shape[1], values.shape[0] * values.shape[2])


def attend_forward(query_heads, key_heads, value_heads, key_valid, score_scale):

    def one_head(head_items):
        query_rows, key_rows, value_rows = head_items
        scores = times_transpose(query_rows, key_rows) * score_scale
        scores = jnp.where(key_valid[None, :], scores, masked_score)
        row_top = jnp.max(scores, axis=1, keepdims=True)
        row_total = jnp.sum(jnp.exp(scores - row_top), axis=1, keepdims=True)
        log_total = row_top + jnp.log(row_total)
        probs_low = jnp.exp(scores - log_total).astype(jnp.bfloat16)
        head_out = jnp.dot(probs_low, value_rows, preferred_element_type=jnp.float32)
        return (head_out, log_total[:, 0])

    return lax.map(one_head, (query_heads, key_heads, value_heads))


def attend_backward(
    query_heads, key_heads, value_heads, log_totals, grad_heads, key_valid, score_scale
):

    def one_head(head_items):
        query_rows, key_rows, value_rows, log_total, grad_rows = head_items
        scores = times_transpose(query_rows, key_rows) * score_scale
        scores = jnp.where(key_valid[None, :], scores, masked_score)
        probs_full = jnp.exp(scores - log_total[:, None])
        grad_probs = times_transpose(grad_rows, value_rows)
        row_delta = jnp.sum(probs_full * grad_probs, axis=1, keepdims=True)
        grad_scores = (probs_full * (grad_probs - row_delta)).astype(jnp.bfloat16)
        grad_query = (
            jnp.dot(grad_scores, key_rows, preferred_element_type=jnp.float32) * score_scale
        )
        grad_key = contract_rows(grad_scores, query_rows) * score_scale
        grad_value = contract_rows(probs_full.astype(jnp.bfloat16), grad_rows)
        return (grad_query, grad_key, grad_value)

    return lax.map(one_head, (query_heads, key_heads, value_heads, log_totals, grad_heads))


def gelu_exact(values):
    return jax.nn.gelu(values, approximate=False)


def local(
    tokens,
    w_query,
    w_key,
    w_value,
    w_output,
    w_inner,
    w_outer,
    first_gain,
    first_shift,
    second_gain,
    second_shift,
    seq_lengths,
    out_grad,
):
    micro_count = tokens.shape[0]
    feat_a = tokens.shape[1]
    rows_a = tokens.shape[2]
    count_col = lax.axis_size("col")
    count_row = lax.axis_size("row")
    seq_total = rows_a * count_col
    rows_b = seq_total // count_row
    full_width = feat_a * count_row
    head_size = HD
    score_scale = head_size ** (-0.5)
    width_b = w_query.shape[1]
    inner_width = w_inner.shape[1]
    group_index = lax.axis_index("dp")
    pos_a = lax.axis_index("col") * rows_a + jnp.arange(rows_a, dtype=jnp.int32)
    pos_b = lax.axis_index("row") * rows_b + jnp.arange(rows_b, dtype=jnp.int32)
    pos_all = jnp.arange(seq_total, dtype=jnp.int32)
    acc_qkv = jnp.zeros((feat_a, 3 * width_b), jnp.float32)
    acc_output = jnp.zeros((width_b, feat_a), jnp.float32)
    acc_inner = jnp.zeros((feat_a, inner_width), jnp.float32)
    acc_outer = jnp.zeros((inner_width, feat_a), jnp.float32)
    acc_gain_one = jnp.zeros((feat_a,), jnp.float32)
    acc_shift_one = jnp.zeros((feat_a,), jnp.float32)
    acc_gain_two = jnp.zeros((feat_a,), jnp.float32)
    acc_shift_two = jnp.zeros((feat_a,), jnp.float32)
    outputs = []
    input_grads = []
    for micro_step in range(micro_count):
        forward_blocks = fetch_blocks(w_query, w_key, w_value, w_output, w_inner, w_outer)
        query_block, key_block, value_block, output_block, inner_block, outer_block = forward_blocks
        length_now = lax.dynamic_index_in_dim(seq_lengths[micro_step], group_index, keepdims=False)
        valid_a = pos_a < length_now
        key_valid = pos_all < length_now
        tokens_now = tokens[micro_step].T
        tokens_all = along_col(tokens_now)
        qkv_block = jnp.concatenate([query_block, key_block, value_block], axis=1)
        projected = reduce_rows(jnp.dot(tokens_all, qkv_block, preferred_element_type=jnp.float32))
        query_rot = rotate_pairs(projected[:, :width_b], pos_b, head_size, 1.0).astype(jnp.bfloat16)
        key_rot = rotate_pairs(projected[:, width_b : 2 * width_b], pos_b, head_size, 1.0).astype(
            jnp.bfloat16
        )
        value_low = projected[:, 2 * width_b :].astype(jnp.bfloat16)
        key_all, value_all = (
            lax.all_gather(key_rot, "row", axis=0, tiled=True),
            lax.all_gather(value_low, "row", axis=0, tiled=True),
        )
        query_heads = split_heads(query_rot, head_size)
        head_outs, log_totals = attend_forward(
            query_heads,
            split_heads(key_all, head_size),
            split_heads(value_all, head_size),
            key_valid,
            score_scale,
        )
        attn_low = merge_heads(head_outs).astype(jnp.bfloat16)
        attn_all = along_row(attn_low)
        branch = reduce_cols(jnp.dot(attn_all, output_block, preferred_element_type=jnp.float32))
        hidden, centered_one, inv_one = layer_norm(
            tokens_now.astype(jnp.float32) + branch, first_gain, first_shift, full_width
        )
        hidden_all = along_col(hidden.astype(jnp.bfloat16))
        inner = reduce_rows(jnp.dot(hidden_all, inner_block, preferred_element_type=jnp.float32))
        act_low = gelu_exact(inner).astype(jnp.bfloat16)
        act_all = along_row(act_low)
        outer = reduce_cols(jnp.dot(act_all, outer_block, preferred_element_type=jnp.float32))
        result, centered_two, inv_two = layer_norm(
            hidden + outer, second_gain, second_shift, full_width
        )
        outputs.append(result.astype(jnp.bfloat16).T)
        backward_blocks = fetch_blocks(w_query, w_key, w_value, w_output, w_inner, w_outer)
        query_back, key_block_back, value_back, output_back, inner_back, outer_back = (
            backward_blocks
        )
        qkv_back = jnp.concatenate([query_back, key_block_back, value_back], axis=1)
        cot_now = out_grad[micro_step].T.astype(jnp.float32) * valid_a[:, None].astype(jnp.float32)
        acc_gain_two = acc_gain_two + jnp.sum(cot_now * centered_two, axis=0)
        acc_shift_two = acc_shift_two + jnp.sum(cot_now, axis=0)
        grad_two = layer_norm_back(cot_now, centered_two, inv_two, second_gain, full_width)
        outer_all = along_col(grad_two.astype(jnp.bfloat16))
        grad_act = reduce_rows(times_transpose(outer_all, outer_back))
        acc_outer = acc_outer + contract_rows(act_all, outer_all)
        gelu_pull = jax.vjp(gelu_exact, inner)[1]
        inner_low = gelu_pull(grad_act)[0].astype(jnp.bfloat16)
        inner_all = along_row(inner_low)
        grad_hidden = grad_two + reduce_cols(times_transpose(inner_all, inner_back))
        acc_inner = acc_inner + contract_rows(hidden_all, inner_all)
        acc_gain_one = acc_gain_one + jnp.sum(grad_hidden * centered_one, axis=0)
        acc_shift_one = acc_shift_one + jnp.sum(grad_hidden, axis=0)
        grad_one = layer_norm_back(grad_hidden, centered_one, inv_one, first_gain, full_width)
        branch_all = along_col(grad_one.astype(jnp.bfloat16))
        grad_attn = reduce_rows(times_transpose(branch_all, output_back))
        acc_output = acc_output + contract_rows(attn_all, branch_all)
        key_again, value_again = (
            lax.all_gather(key_rot, "row", axis=0, tiled=True),
            lax.all_gather(value_low, "row", axis=0, tiled=True),
        )
        grad_q_heads, grad_k_heads, grad_v_heads = attend_backward(
            query_heads,
            split_heads(key_again, head_size),
            split_heads(value_again, head_size),
            log_totals,
            split_heads(grad_attn.astype(jnp.bfloat16), head_size),
            key_valid,
            score_scale,
        )
        key_sum, value_sum = (
            lax.psum_scatter(
                merge_heads(grad_k_heads).astype(jnp.bfloat16),
                "row",
                scatter_dimension=0,
                tiled=True,
            ).astype(jnp.float32),
            lax.psum_scatter(
                merge_heads(grad_v_heads).astype(jnp.bfloat16),
                "row",
                scatter_dimension=0,
                tiled=True,
            ).astype(jnp.float32),
        )
        grad_query = rotate_pairs(merge_heads(grad_q_heads), pos_b, head_size, -1.0).astype(
            jnp.bfloat16
        )
        grad_key = rotate_pairs(key_sum, pos_b, head_size, -1.0).astype(jnp.bfloat16)
        grad_value = value_sum.astype(jnp.bfloat16)
        proj_all = along_row(jnp.concatenate([grad_query, grad_key, grad_value], axis=1))
        input_grads.append((grad_one + reduce_cols(times_transpose(proj_all, qkv_back))).T)
        acc_qkv = acc_qkv + contract_rows(tokens_all, proj_all)
    grad_parts = (
        lax.psum_scatter(
            acc_qkv[:, :width_b].astype(jnp.bfloat16), "dp", scatter_dimension=0, tiled=True
        ).astype(jnp.float32),
        lax.psum_scatter(
            acc_qkv[:, width_b : 2 * width_b].astype(jnp.bfloat16),
            "dp",
            scatter_dimension=0,
            tiled=True,
        ).astype(jnp.float32),
        lax.psum_scatter(
            acc_qkv[:, 2 * width_b :].astype(jnp.bfloat16), "dp", scatter_dimension=0, tiled=True
        ).astype(jnp.float32),
        lax.psum_scatter(
            acc_output.astype(jnp.bfloat16), "dp", scatter_dimension=0, tiled=True
        ).astype(jnp.float32),
        lax.psum_scatter(
            acc_inner.astype(jnp.bfloat16), "dp", scatter_dimension=0, tiled=True
        ).astype(jnp.float32),
        lax.psum_scatter(
            acc_outer.astype(jnp.bfloat16), "dp", scatter_dimension=0, tiled=True
        ).astype(jnp.float32),
    )
    norm_parts = lax.psum((acc_gain_one, acc_shift_one, acc_gain_two, acc_shift_two), ("dp", "col"))
    return (
        jnp.stack(outputs),
        jnp.stack(input_grads),
        grad_parts[0],
        grad_parts[1],
        grad_parts[2],
        grad_parts[3],
        grad_parts[4],
        grad_parts[5],
        norm_parts[0],
        norm_parts[1],
        norm_parts[2],
        norm_parts[3],
    )


def solution(mesh):
    placed = (
        P(None, "row", ("dp", "col")),
        P(("row", "dp"), "col"),
        P(("row", "dp"), "col"),
        P(("row", "dp"), "col"),
        P(("col", "dp"), "row"),
        P(("row", "dp"), "col"),
        P(("col", "dp"), "row"),
        P("row"),
        P("row"),
        P("row"),
        P("row"),
        P(),
        P(None, "row", ("dp", "col")),
    )
    return jax.shard_map(
        local,
        mesh=mesh,
        in_specs=placed,
        out_specs=(
            P(None, "row", ("dp", "col")),
            P(None, "row", ("dp", "col")),
            P(("row", "dp"), "col"),
            P(("row", "dp"), "col"),
            P(("row", "dp"), "col"),
            P(("col", "dp"), "row"),
            P(("row", "dp"), "col"),
            P(("col", "dp"), "row"),
            P("row"),
            P("row"),
            P("row"),
            P("row"),
        ),
        check_vma=False,
    )
```

profile of v0, /device:TPU:0, one launch (start us, length us, event | category | flops | bytes accessed | tf_op | source)
XLA Modules:
  0.0 1733.2 jit_solution(12513818273407900545)
XLA Ops:
  24.2 9.1 all_gather.103
  36.5 8.7 all_gather.112
  56.4 65.9 %reduce-scatter.29.cloned.1.call-done = f32[512,576]{0,1:T(8,128)} async-done(((f32[2048,576]{0,1:T(8,128)}), f32[512,576]{0,1:T(8,128)}) %reduce-scatter.29.cloned.1.call-update) | async-done | bytes 1179664 | tf_op jit(solution)/shard_map/reduce_scatter | solution.py:49
  124.9 28.4 %all_gather.105 = bf16[2048,192]{0,1:T(8,128)(2,1)S(1)} all-gather(bf16[512,192]{0,1:T(8,128)(2,1)S(1)} %slice.241), channel_id=1, replica_groups=mesh['dp'=2,'row'=4,'col'=4] {'row'}, dimensions={0}, use_global_device_ids=true | all-gather | bytes 983040 | tf_op jit(solution)/shard_map/all_gather | solution.py:204
  154.9 64.5 %reduce-scatter.37.cloned.1.call-done = f32[512,576]{0,1:T(8,128)} async-done(((f32[2048,576]{0,1:T(8,128)}), f32[512,576]{0,1:T(8,128)}) %reduce-scatter.37.cloned.1.call-update) | async-done | bytes 1179664 | tf_op jit(solution)/shard_map/reduce_scatter | solution.py:49
  226.7 20.1 %all_gather.104 = bf16[2048,192]{0,1:T(8,128)(2,1)} all-gather(bf16[512,192]{0,1:T(8,128)(2,1)S(1)} %convert_element_type.287), channel_id=1, replica_groups=mesh['dp'=2,'row'=4,'col'=4] {'row'}, dimensions={0}, use_global_device_ids=true | all-gather | bytes 983040 | tf_op jit(solution)/shard_map/all_gather | solution.py:203
  246.8 17.5 %all_gather.113 = bf16[2048,192]{0,1:T(8,128)(2,1)S(1)} all-gather(bf16[512,192]{0,1:T(8,128)(2,1)S(1)} %convert_element_type.300), channel_id=1, replica_groups=mesh['dp'=2,'row'=4,'col'=4] {'row'}, dimensions={0}, use_global_device_ids=true | all-gather | bytes 983040 | tf_op jit(solution)/shard_map/all_gather | solution.py:203
  265.2 17.3 %all_gather.114 = bf16[2048,192]{0,1:T(8,128)(2,1)} all-gather(bf16[512,192]{0,1:T(8,128)(2,1)S(1)} %slice.240), channel_id=1, replica_groups=mesh['dp'=2,'row'=4,'col'=4] {'row'}, dimensions={0}, use_global_device_ids=true | all-gather | bytes 983040 | tf_op jit(solution)/shard_map/all_gather | solution.py:204
  285.2 15.3 while.56
  300.6 16.6 all_gather.106
  323.0 15.5 while.57
  339.0 15.8 all_gather.115
  365.2 17.0 reduce-scatter.39.cloned.1.call-done
  384.0 12.5 all-reduce.4
  410.6 109.0 %reduce-scatter.33.cloned.1.call-done = f32[512,768]{1,0:T(8,128)} async-done(((f32[2048,768]{1,0:T(8,128)}), f32[512,768]{1,0:T(8,128)}) %reduce-scatter.33.cloned.1.call-update) | async-done | bytes 1572880 | tf_op jit(solution)/shard_map/reduce_scatter | solution.py:49
  525.2 7.9 all_gather.111
  533.1 56.2 %all-gather.7.cloned.1.call-done = bf16[2048,768]{1,0:T(8,128)(2,1)} async-done(((bf16[512,768]{1,0:T(8,128)(2,1)}), bf16[2048,768]{1,0:T(8,128)(2,1)}) %all-gather.7.cloned.1.call-update) | async-done | bytes 3145744 | tf_op jit(solution)/shard_map/all_gather | solution.py:45
  594.1 21.3 %reduce-scatter.35.cloned.1.call-done = bf16[512,192]{0,1:T(8,128)(2,1)} async-done(((bf16[2048,192]{0,1:T(8,128)(2,1)}), bf16[512,192]{0,1:T(8,128)(2,1)}) %reduce-scatter.35.cloned.1.call-update) | async-done | bytes 196624 | tf_op jit(solution)/shard_map/reduce_scatter | solution.py:53
  618.1 8.2 all_gather.116
  631.0 111.2 %reduce-scatter.41.cloned.1.call-done = f32[512,768]{1,0:T(8,128)} async-done(((f32[2048,768]{1,0:T(8,128)}), f32[512,768]{1,0:T(8,128)}) %reduce-scatter.41.cloned.1.call-update) | async-done | bytes 1572880 | tf_op jit(solution)/shard_map/reduce_scatter | solution.py:49
  748.0 63.9 %all-gather.9.cloned.1.call-done = bf16[2048,768]{1,0:T(8,128)(2,1)} async-done(((bf16[512,768]{1,0:T(8,128)(2,1)}), bf16[2048,768]{1,0:T(8,128)(2,1)}) %all-gather.9.cloned.1.call-update) | async-done | bytes 3145744 | tf_op jit(solution)/shard_map/all_gather | solution.py:45
  817.8 20.1 %reduce-scatter.43.cloned.1.call-done = bf16[512,192]{0,1:T(8,128)(2,1)} async-done(((bf16[2048,192]{0,1:T(8,128)(2,1)}), bf16[512,192]{0,1:T(8,128)(2,1)}) %reduce-scatter.43.cloned.1.call-update) | async-done | bytes 196624 | tf_op jit(solution)/shard_map/reduce_scatter | solution.py:53
  840.5 12.5 all-reduce.3
  856.7 9.2 all-reduce.2
  883.5 8.9 all_gather.118
  898.0 96.0 %reduce-scatter.57.cloned.1.call-done = f32[512,768]{1,0:T(8,128)} async-done(((f32[2048,768]{1,0:T(8,128)}), f32[512,768]{1,0:T(8,128)}) %reduce-scatter.57.cloned.1.call-update) | async-done | bytes 1572880 | tf_op jit(solution)/shard_map/reduce_scatter | solution.py:49
  997.9 109.5 %reduce-scatter.45.cloned.1.call-done = f32[512,768]{1,0:T(8,128)} async-done(((f32[2048,768]{1,0:T(8,128)}), f32[512,768]{1,0:T(8,128)}) %reduce-scatter.45.cloned.1.call-update) | async-done | bytes 1572880 | tf_op jit(solution)/shard_map/reduce_scatter | solution.py:49
  1111.4 62.2 %all-gather.15.cloned.1.call-done = bf16[2048,768]{1,0:T(8,128)(2,1)} async-done(((bf16[512,768]{1,0:T(8,128)(2,1)}), bf16[2048,768]{1,0:T(8,128)(2,1)}) %all-gather.15.cloned.1.call-update) | async-done | bytes 3145744 | tf_op jit(solution)/shard_map/all_gather | solution.py:45
  1177.6 59.6 %all-gather.11.cloned.1.call-done = bf16[2048,768]{1,0:T(8,128)(2,1)} async-done(((bf16[512,768]{1,0:T(8,128)(2,1)}), bf16[2048,768]{1,0:T(8,128)(2,1)}) %all-gather.11.cloned.1.call-update) | async-done | bytes 3145744 | tf_op jit(solution)/shard_map/all_gather | solution.py:45
  1241.3 20.8 %reduce-scatter.59.cloned.1.call-done = bf16[512,192]{0,1:T(8,128)(2,1)} async-done(((bf16[2048,192]{0,1:T(8,128)(2,1)}), bf16[512,192]{0,1:T(8,128)(2,1)}) %reduce-scatter.59.cloned.1.call-update) | async-done | bytes 196624 | tf_op jit(solution)/shard_map/reduce_scatter | solution.py:53
  1262.1 25.9 %reduce-scatter.47.cloned.1.call-done = bf16[512,192]{0,1:T(8,128)(2,1)} async-done(((bf16[2048,192]{0,1:T(8,128)(2,1)}), bf16[512,192]{0,1:T(8,128)(2,1)}) %reduce-scatter.47.cloned.1.call-update) | async-done | bytes 196624 | tf_op jit(solution)/shard_map/reduce_scatter | solution.py:53
  1291.6 12.5 all-reduce.1
  1319.2 8.9 all_gather.120
  1331.9 20.8 %reduce-scatter.61.cloned.1.call-done = f32[512,192]{0,1:T(8,128)} async-done(((f32[2048,192]{0,1:T(8,128)}), f32[512,192]{0,1:T(8,128)}) %reduce-scatter.61.cloned.1.call-update) | async-done | bytes 393232 | tf_op jit(solution)/shard_map/reduce_scatter | solution.py:49
  1359.1 30.5 %while.59 = (s32[]{:T(128)}, f32[3,512,64]{1,2,0:T(8,128)}, bf16[3,2048,64]{1,2,0:T(8,128)(2,1)}, bf16[3,2048,64]{1,2,0:T(8,128)(2,1)}, bf16[3,512,64]{2,1,0:T(8...) while((s32[]{:T(128)}, f32[3,512,64]{1,2,0:T(8,128)}, ...), condition=%wide.region_62.63_spmd.clone, body=%wide.region_60.62_spmd.clone.sunk | while | flops 680691200 | bytes 48123144 | solution.py:139
  1392.8 25.2 %while.58 = (s32[]{:T(128)}, f32[3,512,64]{1,2,0:T(8,128)}, bf16[3,2048,64]{1,2,0:T(8,128)(2,1)}, bf16[3,2048,64]{1,2,0:T(8,128)(2,1)S(1)}, bf16[3,512,64]{2,1,0...) while((s32[]{:T(128)}, f32[3,512,64]{1,2,0:T(8,128)}, ...), condition=%wide.region_45.46_spmd.clone, body=%wide.region_43.45_spmd.clone.sunk | while | flops 680691200 | bytes 41045172 | solution.py:139
  1421.4 19.2 %reduce-scatter.51.cloned.1.call-done = bf16[512,192]{0,1:T(8,128)(2,1)} async-done(((bf16[2048,192]{0,1:T(8,128)(2,1)}), bf16[512,192]{0,1:T(8,128)(2,1)}) %reduce-scatter.51.cloned.1.call-update) | async-done | bytes 196624 | tf_op jit(solution)/shard_map/reduce_scatter | solution.py:266
  1446.0 19.5 %reduce-scatter.53.cloned.1.call-done = bf16[512,192]{0,1:T(8,128)(2,1)} async-done(((bf16[2048,192]{0,1:T(8,128)(2,1)}), bf16[512,192]{0,1:T(8,128)(2,1)}) %reduce-scatter.53.cloned.1.call-update) | async-done | bytes 196624 | tf_op jit(solution)/shard_map/reduce_scatter | solution.py:272
  1468.7 21.8 %reduce-scatter.65.cloned.1.call-done = bf16[512,192]{0,1:T(8,128)(2,1)} async-done(((bf16[2048,192]{0,1:T(8,128)(2,1)}), bf16[512,192]{0,1:T(8,128)(2,1)}) %reduce-scatter.65.cloned.1.call-update) | async-done | bytes 196624 | tf_op jit(solution)/shard_map/reduce_scatter | solution.py:272
  1504.6 37.7 %all-gather.13.cloned.1.call-done = bf16[2048,576]{0,1:T(8,128)(2,1)} async-done(((bf16[512,576]{0,1:T(8,128)(2,1)}), bf16[2048,576]{0,1:T(8,128)(2,1)}) %all-gather.13.cloned.1.call-update) | async-done | bytes 2359312 | tf_op jit(solution)/shard_map/all_gather | solution.py:45
  1545.0 48.1 %all-gather.17.cloned.1.call-done = bf16[2048,576]{0,1:T(8,128)(2,1)} async-done(((bf16[512,576]{0,1:T(8,128)(2,1)}), bf16[2048,576]{0,1:T(8,128)(2,1)}) %all-gather.17.cloned.1.call-update) | async-done | bytes 2359312 | tf_op jit(solution)/shard_map/all_gather | solution.py:45
  1609.1 13.0 reduce-scatter.77.cloned.1.call-done
  1623.8 13.3 all-reduce
  1638.6 8.6 reduce-scatter.69.cloned.1.call-done
  1648.6 10.9 reduce-scatter.71.cloned.1.call-done
  1660.9 10.7 reduce-scatter.73.cloned.1.call-done
  1673.1 25.1 %reduce-scatter.55.cloned.1.call-done = bf16[512,192]{0,1:T(8,128)(2,1)} async-done(((bf16[2048,192]{0,1:T(8,128)(2,1)}), bf16[512,192]{0,1:T(8,128)(2,1)}) %reduce-scatter.55.cloned.1.call-update) | async-done | bytes 196624 | tf_op jit(solution)/shard_map/reduce_scatter | solution.py:53
  1698.2 25.9 %reduce-scatter.67.cloned.1.call-done = bf16[512,192]{0,1:T(8,128)(2,1)} async-done(((bf16[2048,192]{0,1:T(8,128)(2,1)}), bf16[512,192]{0,1:T(8,128)(2,1)}) %reduce-scatter.67.cloned.1.call-update) | async-done | bytes 196624 | tf_op jit(solution)/shard_map/reduce_scatter | solution.py:53
  (487 shorter events, 325.4 us)
Async XLA Ops:
  7.2 115.1 %reduce-scatter.29.cloned.1.call-start = ((), (), s32[]{:S(2)}) async-start(), calls=%async_computation.26 | async-start | bytes 5898240 | tf_op jit(solution)/shard_map/reduce_scatter | solution.py:49
  36.5 182.9 %reduce-scatter.37.cloned.1.call-start = ((), (), s32[]{:S(2)}) async-start(), calls=%async_computation.31 | async-start | bytes 5898240 | tf_op jit(solution)/shard_map/reduce_scatter | solution.py:49
  48.4 316.8 %reduce-scatter.31.cloned.1.call-start = ((), (), s32[]{:S(2)}) async-start(), calls=%async_computation.27 | async-start | bytes 983040 | tf_op jit(solution)/shard_map/reduce_scatter | solution.py:53
  48.5 75.4 %copy-start.49 = (bf16[3,512,64]{1,2,0:T(8,128)(2,1)}, bf16[3,512,64]{1,2,0:T(8,128)(2,1)S(1)}, u32[]{:S(2)}) copy-start(bf16[3,512,64]{1,2,0:T(8,128)(2,1)S(1)} %fusion.145) | copy-start | bytes 589828
  56.4 164.7 %copy-start.55 = (f32[512,32]{0,1:T(8,128)}, f32[512,32]{0,1:T(8,128)S(1)}, u32[]{:S(2)}) copy-start(f32[512,32]{0,1:T(8,128)S(1)} %get-tuple-element.541) | copy-start | bytes 196612
  320.3 61.9 %reduce-scatter.39.cloned.1.call-start = ((), (), s32[]{:S(2)}) async-start(), calls=%async_computation.32 | async-start | bytes 983040 | tf_op jit(solution)/shard_map/reduce_scatter | solution.py:53
  355.7 41.5 %copy-start.77 = (f32[192]{0:T(256)S(1)}, f32[192]{0:T(256)}, u32[]{:S(2)}) copy-start(f32[192]{0:T(256)} %param.29) | copy-start | bytes 2308
  358.0 161.6 %reduce-scatter.33.cloned.1.call-start = ((), (), s32[]{:S(2)}) async-start(), calls=%async_computation.28 | async-start | bytes 7864320 | tf_op jit(solution)/shard_map/reduce_scatter | solution.py:49
  410.6 178.7 %all-gather.7.cloned.1.call-start = ((), (), s32[]{:S(2)}) async-start(), calls=%async_computation.29 | async-start | bytes 3932160 | tf_op jit(solution)/shard_map/all_gather | solution.py:45
  525.1 90.2 %reduce-scatter.35.cloned.1.call-start = ((), (), s32[]{:S(2)}) async-start(), calls=%async_computation.30 | async-start | bytes 983040 | tf_op jit(solution)/shard_map/reduce_scatter | solution.py:53
  593.3 148.9 %reduce-scatter.41.cloned.1.call-start = ((), (), s32[]{:S(2)}) async-start(), calls=%async_computation.33 | async-start | bytes 7864320 | tf_op jit(solution)/shard_map/reduce_scatter | solution.py:49
  630.9 181.0 %all-gather.9.cloned.1.call-start = ((), (), s32[]{:S(2)}) async-start(), calls=%async_computation.34 | async-start | bytes 3932160 | tf_op jit(solution)/shard_map/all_gather | solution.py:45
  747.7 90.2 %reduce-scatter.43.cloned.1.call-start = ((), (), s32[]{:S(2)}) async-start(), calls=%async_computation.35 | async-start | bytes 983040 | tf_op jit(solution)/shard_map/reduce_scatter | solution.py:53
  815.8 178.1 %reduce-scatter.57.cloned.1.call-start = ((), (), s32[]{:S(2)}) async-start(), calls=%async_computation.44 | async-start | bytes 7864320 | tf_op jit(solution)/shard_map/reduce_scatter | solution.py:49
  883.4 224.0 %reduce-scatter.45.cloned.1.call-start = ((), (), s32[]{:S(2)}) async-start(), calls=%async_computation.36 | async-start | bytes 7864320 | tf_op jit(solution)/shard_map/reduce_scatter | solution.py:49
  897.9 275.7 %all-gather.15.cloned.1.call-start = ((), (), s32[]{:S(2)}) async-start(), calls=%async_computation.45 | async-start | bytes 3932160 | tf_op jit(solution)/shard_map/all_gather | solution.py:45
  997.8 239.4 %all-gather.11.cloned.1.call-start = ((), (), s32[]{:S(2)}) async-start(), calls=%async_computation.37 | async-start | bytes 3932160 | tf_op jit(solution)/shard_map/all_gather | solution.py:45
  1111.3 150.8 %reduce-scatter.59.cloned.1.call-start = ((), (), s32[]{:S(2)}) async-start(), calls=%async_computation.46 | async-start | bytes 983040 | tf_op jit(solution)/shard_map/reduce_scatter | solution.py:53
  1177.6 110.3 %reduce-scatter.47.cloned.1.call-start = ((), (), s32[]{:S(2)}) async-start(), calls=%async_computation.38 | async-start | bytes 983040 | tf_op jit(solution)/shard_map/reduce_scatter | solution.py:53
  1241.2 111.6 %reduce-scatter.61.cloned.1.call-start = ((), (), s32[]{:S(2)}) async-start(), calls=%async_computation.47 | async-start | bytes 1966080 | tf_op jit(solution)/shard_map/reduce_scatter | solution.py:49
  1319.1 70.5 %reduce-scatter.49.cloned.1.call-start = ((), (), s32[]{:S(2)}) async-start(), calls=%async_computation.39 | async-start | bytes 1966080 | tf_op jit(solution)/shard_map/reduce_scatter | solution.py:49
  1331.5 88.7 %reduce-scatter.63.cloned.1.call-start = ((), (), s32[]{:S(2)}) async-start(), calls=%async_computation.48 | async-start | bytes 983040 | tf_op jit(solution)/shard_map/reduce_scatter | solution.py:266
  1389.6 51.0 %reduce-scatter.51.cloned.1.call-start = ((), (), s32[]{:S(2)}) async-start(), calls=%async_computation.40 | async-start | bytes 983040 | tf_op jit(solution)/shard_map/reduce_scatter | solution.py:266
  1418.0 47.5 %reduce-scatter.53.cloned.1.call-start = ((), (), s32[]{:S(2)}) async-start(), calls=%async_computation.41 | async-start | bytes 983040 | tf_op jit(solution)/shard_map/reduce_scatter | solution.py:272
  1418.9 71.5 %reduce-scatter.65.cloned.1.call-start = ((), (), s32[]{:S(2)}) async-start(), calls=%async_computation.49 | async-start | bytes 983040 | tf_op jit(solution)/shard_map/reduce_scatter | solution.py:272
  1419.7 122.6 %all-gather.13.cloned.1.call-start = ((), (), s32[]{:S(2)}) async-start(), calls=%async_computation.42 | async-start | bytes 2949120 | tf_op jit(solution)/shard_map/all_gather | solution.py:45
  1467.3 125.8 %all-gather.17.cloned.1.call-start = ((), (), s32[]{:S(2)}) async-start(), calls=%async_computation.50 | async-start | bytes 2949120 | tf_op jit(solution)/shard_map/all_gather | solution.py:45
  1492.3 115.1 %reduce-scatter.79.cloned.1.call-start = ((), (), s32[]{:S(2)}) async-start(), calls=%async_computation.57 | async-start | bytes 589824
  1497.1 125.0 %reduce-scatter.77.cloned.1.call-start = ((), (), s32[]{:S(2)}) async-start(), calls=%async_computation.56 | async-start | bytes 442368 | tf_op jit(solution)/shard_map/reduce_scatter | solution.py:303
  1502.2 134.9 %reduce-scatter.75.cloned.1.call-start = ((), (), s32[]{:S(2)}) async-start(), calls=%async_computation.55 | async-start | bytes 147456 | tf_op jit(solution)/shard_map/reduce_scatter | solution.py:300
  1504.6 88.5 %copy-start.30 = (bf16[2048,192]{0,1:T(8,128)(2,1)S(1)}, bf16[2048,192]{0,1:T(8,128)(2,1)}, u32[]{:S(2)}) copy-start(bf16[2048,192]{0,1:T(8,128)(2,1)} %copy-done.29) | copy-start | bytes 2359300
  1504.6 142.6 %reduce-scatter.69.cloned.1.call-start = ((), (), s32[]{:S(2)}) async-start(), calls=%async_computation.52 | async-start | bytes 147456 | tf_op jit(solution)/shard_map/reduce_scatter | solution.py:288
  1545.0 53.0 %copy-start.42 = (bf16[192,192]{1,0:T(8,128)(2,1)S(1)}, bf16[192,192]{1,0:T(8,128)(2,1)}, u32[]{:S(2)}) copy-start(bf16[192,192]{1,0:T(8,128)(2,1)} %copy-done.41) | copy-start | bytes 221188
  1545.0 53.0 %copy-start.44 = (bf16[192,192]{1,0:T(8,128)(2,1)S(1)}, bf16[192,192]{1,0:T(8,128)(2,1)}, u32[]{:S(2)}) copy-start(bf16[192,192]{1,0:T(8,128)(2,1)} %copy-done.43) | copy-start | bytes 221188
  1545.0 53.0 %copy-start.46 = (bf16[192,192]{1,0:T(8,128)(2,1)S(1)}, bf16[192,192]{1,0:T(8,128)(2,1)}, u32[]{:S(2)}) copy-start(bf16[192,192]{1,0:T(8,128)(2,1)} %copy-done.45) | copy-start | bytes 221188
  1596.6 62.9 %reduce-scatter.71.cloned.1.call-start = ((), (), s32[]{:S(2)}) async-start(), calls=%async_computation.53 | async-start | bytes 147456 | tf_op jit(solution)/shard_map/reduce_scatter | solution.py:291
  1597.4 74.3 %reduce-scatter.73.cloned.1.call-start = ((), (), s32[]{:S(2)}) async-start(), calls=%async_computation.54 | async-start | bytes 147456 | tf_op jit(solution)/shard_map/reduce_scatter | solution.py:297
  1598.0 100.3 %reduce-scatter.55.cloned.1.call-start = ((), (), s32[]{:S(2)}) async-start(), calls=%async_computation.43 | async-start | bytes 983040 | tf_op jit(solution)/shard_map/reduce_scatter | solution.py:53
  1601.6 122.5 %reduce-scatter.67.cloned.1.call-start = ((), (), s32[]{:S(2)}) async-start(), calls=%async_computation.51 | async-start | bytes 983040 | tf_op jit(solution)/shard_map/reduce_scatter | solution.py:53
  1603.4 120.6 %copy-start.20 = (bf16[512,192]{0,1:T(8,128)(2,1)S(1)}, bf16[512,192]{0,1:T(8,128)(2,1)}, u32[]{:S(2)}) copy-start(bf16[512,192]{0,1:T(8,128)(2,1)} %reduce-scatter.31.cloned.1.call-done) | copy-start | bytes 589828
  1603.4 120.6 %copy-start.21 = (bf16[512,192]{0,1:T(8,128)(2,1)S(1)}, bf16[512,192]{0,1:T(8,128)(2,1)}, u32[]{:S(2)}) copy-start(bf16[512,192]{0,1:T(8,128)(2,1)} %reduce-scatter.39.cloned.1.call-done) | copy-start | bytes 589828
  1603.5 120.6 %copy-start.23 = (f32[512,192]{0,1:T(8,128)S(1)}, f32[512,192]{0,1:T(8,128)}, u32[]{:S(2)}) copy-start(f32[512,192]{0,1:T(8,128)} %get-tuple-element.473) | copy-start | bytes 1179652
  1603.5 120.6 %copy-start.24 = (f32[512,192]{0,1:T(8,128)S(1)}, f32[512,192]{0,1:T(8,128)}, u32[]{:S(2)}) copy-start(f32[512,192]{0,1:T(8,128)} %get-tuple-element.474) | copy-start | bytes 1179652
  1603.5 120.6 %copy-start.60 = (f32[192]{0:T(256)S(1)}, f32[192]{0:T(256)}, u32[]{:S(2)}) copy-start(f32[192]{0:T(256)} %param.28) | copy-start | bytes 2308
  1603.5 120.6 %copy-start.66 = (f32[512]{0:T(512)S(1)}, f32[512]{0:T(512)}, u32[]{:S(2)}) copy-start(f32[512]{0:T(512)} %copy-done.65) | copy-start | bytes 6148
  1603.5 120.6 %copy-start.68 = (f32[512]{0:T(512)S(1)}, f32[512]{0:T(512)}, u32[]{:S(2)}) copy-start(f32[512]{0:T(512)} %copy-done.67) | copy-start | bytes 6148
  1603.5 120.6 %copy-start.70 = (f32[512]{0:T(512)S(1)}, f32[512]{0:T(512)}, u32[]{:S(2)}) copy-start(f32[512]{0:T(512)} %copy-done.69) | copy-start | bytes 6148
  1603.5 120.6 %copy-start.72 = (f32[512]{0:T(512)S(1)}, f32[512]{0:T(512)}, u32[]{:S(2)}) copy-start(f32[512]{0:T(512)} %copy-done.71) | copy-start | bytes 6148
  (85 other events, 536.0 us)
Sparse Core Ops, SparseCore 0:
  36.6 85.5 reduce-scatter.28
  124.5 94.8 reduce-scatter.36
  320.4 24.0 reduce-scatter.30
  358.1 24.0 reduce-scatter.38
  410.7 108.8 reduce-scatter.32
  525.3 63.9 all-gather.6
  593.4 21.8 reduce-scatter.34
  631.0 111.1 reduce-scatter.40
  747.8 63.9 all-gather.8
  816.0 21.9 reduce-scatter.42
  883.5 110.3 reduce-scatter.56
  996.1 111.2 reduce-scatter.44
  1109.5 64.0 all-gather.14
  1175.0 62.1 all-gather.10
  1240.2 21.8 reduce-scatter.58
  1264.6 23.2 reduce-scatter.46
  1319.3 33.4 reduce-scatter.60
  1354.9 34.2 reduce-scatter.48
  1391.5 22.2 reduce-scatter.62
  1418.2 22.4 reduce-scatter.50
  1442.9 22.5 reduce-scatter.52
  1467.8 22.5 reduce-scatter.64
  1492.6 49.6 all-gather.12
  1543.7 49.3 all-gather.16
  1595.3 11.9 reduce-scatter.78
  1610.1 12.0 reduce-scatter.76
  1624.3 9.9 reduce-scatter.74
  1637.2 9.9 reduce-scatter.68
  1649.5 9.9 reduce-scatter.70
  1661.6 9.9 reduce-scatter.72
  1674.9 23.2 reduce-scatter.54
  1700.8 23.2 reduce-scatter.66
where the time goes:
time: 1740 us; the launch traced here: 1730 us
  waiting for transfers between devices  1170 us (67%)
  blocking collectives  278 us (16%)
  matrix products  123 us (7%)
  other arithmetic  93 us (5%)
  local copies, waits for them, and re-layouts  54.1 us (3%)
    reduce_scatter x8, waiting for transfers between devices, reduce_rows(): return lax.psum_scatter(values, 'row', scatter_dimension=0, tiled=True)  577 us
    all_gather x6, waiting for transfers between devices, along_row(): return lax.all_gather(values, 'row', axis=0, tiled=True)  328 us
    reduce_scatter x8, waiting for transfers between devices, reduce_cols(): lax.psum_scatter(values.astype(jnp.bfloat16), 'col', scatter_dimension=0,...  156 us
    all_gather x8, blocking collectives, along_col(): return lax.all_gather(values, 'col', axis=0, tiled=True)  66.9 us
    dot_general x26, matrix products, times_transpose(): lax.dot_general(left, right, (((1,), (1,)), ((), ())), preferred_element_...  52.3 us
    psum x4, blocking collectives, feature_totals(): return lax.psum((first_sum, second_sum), 'row')  46.8 us
    all_gather x2, blocking collectives, local(): lax.all_gather(value_low, 'row', axis=0, tiled=True)  45.8 us
    reduce_scatter x2, waiting for transfers between devices, local(): lax.psum_scatter(merge_heads(grad_v_heads).astype(jnp.bfloat16), 'row', s...  41.3 us
  transfers between devices with their start and end apart: 32, of which 28 were waited for; matrix products, arithmetic and copies ran while one was open for 9% of the time, Pallas kernels for 0%

commit v1 on v0

--- a/solution.py
+++ b/solution.py
@@ -1,3 +1,4 @@
+import functools
 import jax
 import jax.numpy as jnp
 from jax import lax
@@ -6,6 +7,32 @@
 HD = 64
 norm_eps = 1e-05
 masked_score = -1e30
+
+
+def reach_slot(t0, d_out):
+    t0 = jnp.moveaxis(t0, 0, d_out)
+    near = t0.shape
+    return t0.reshape(*near[:d_out], near[d_out] * near[d_out + 1], *near[d_out + 2 :])
+
+
+def fix_group(u_in, net_axis):
+    raw_out, x_now = (lax.axis_size(net_axis), lax.axis_index(net_axis))
+    e_next, aux = (u_in[None], 1)
+    while aux < raw_out:
+        carry_out = lax.ppermute(e_next, net_axis, [(k, k ^ aux) for k in range(raw_out)])
+        vec_out = x_now & aux == 0
+        e_next = jnp.concatenate(
+            [jnp.where(vec_out, e_next, carry_out), jnp.where(vec_out, carry_out, e_next)]
+        )
+        aux *= 2
+    return e_next
+
+
+def choose_circles_up(original, vec, ndim_at):
+    return reach_slot(fix_group(original, vec), ndim_at)
+
+
+process_block_up = functools.partial(choose_circles_up, vec="row", ndim_at=0)
 
 
 def rotate_pairs(values, positions, head_size, direction):
@@ -201,7 +228,7 @@
         value_low = projected[:, 2 * width_b :].astype(jnp.bfloat16)
         key_all, value_all = (
             lax.all_gather(key_rot, "row", axis=0, tiled=True),
-            lax.all_gather(value_low, "row", axis=0, tiled=True),
+            process_block_up(value_low),
         )
         query_heads = split_heads(query_rot, head_size)
         head_outs, log_totals = attend_forward(

time: 1740 us -> 1800 us (1.034)
  blocking collectives: 278 us -> 310 us
    all_gather x2, blocking collectives: 37.5 us -> 58.8 us  [local(): lax.all_gather(key_rot, 'row', axis=0, tiled=True)]
  transfers between devices with their start and end apart: 32 -> 36, of which waited for: 28 -> 27; matrix products, arithmetic and copies ran while one was open for 9% -> 10% of each run, Pallas kernels for 0% -> 0%
where the time goes in v1:
time: 1800 us; the launch traced here: 1790 us
  waiting for transfers between devices  1160 us (64%)
  blocking collectives  310 us (17%)
  matrix products  122 us (7%)
  other arithmetic  99 us (6%)
  local copies, waits for them, and re-layouts  70.3 us (4%)
    reduce_scatter x8, waiting for transfers between devices, reduce_rows(): return lax.psum_scatter(values, 'row', scatter_dimension=0, tiled=True)  574 us
    all_gather x6, waiting for transfers between devices, along_row(): return lax.all_gather(values, 'row', axis=0, tiled=True)  328 us
    reduce_scatter x8, waiting for transfers between devices, reduce_cols(): lax.psum_scatter(values.astype(jnp.bfloat16), 'col', scatter_dimension=0,...  154 us
    all_gather x8, blocking collectives, along_col(): return lax.all_gather(values, 'col', axis=0, tiled=True)  66.7 us
    all_gather x2, blocking collectives, local(): lax.all_gather(key_rot, 'row', axis=0, tiled=True)  58.8 us
    dot_general x26, matrix products, times_transpose(): lax.dot_general(left, right, (((1,), (1,)), ((), ())), preferred_element_...  52.5 us
    all_gather x2, blocking collectives, local(): lax.all_gather(value_low, 'row', axis=0, tiled=True)  52.4 us
    psum x4, blocking collectives, feature_totals(): return lax.psum((first_sum, second_sum), 'row')  46.8 us
  transfers between devices with their start and end apart: 36, of which 27 were waited for; matrix products, arithmetic and copies ran while one was open for 10% of the time, Pallas kernels for 0%

profile of v1, /device:TPU:0, one launch (start us, length us, event | category | flops | bytes accessed | tf_op | source)
XLA Modules:
  0.0 1788.6 jit_solution(719556727810100772)
XLA Ops:
  24.2 9.1 all_gather.101
  36.5 8.7 all_gather.109
  56.2 66.0 %reduce-scatter.29.cloned.1.call-done = f32[512,576]{0,1:T(8,128)} async-done(((f32[2048,576]{0,1:T(8,128)}), f32[512,576]{0,1:T(8,128)}) %reduce-scatter.29.cloned.1.call-update) | async-done | bytes 1179664 | tf_op jit(solution)/shard_map/reduce_scatter | solution.py:76
  127.0 83.3 %reduce-scatter.37.cloned.1.call-done = f32[512,576]{0,1:T(8,128)} async-done(((f32[2048,576]{0,1:T(8,128)}), f32[512,576]{0,1:T(8,128)}) %reduce-scatter.37.cloned.1.call-update) | async-done | bytes 1179664 | tf_op jit(solution)/shard_map/reduce_scatter | solution.py:76
  219.2 19.2 %all_gather.110 = bf16[2048,192]{0,1:T(8,128)(2,1)S(1)} all-gather(bf16[512,192]{0,1:T(8,128)(2,1)S(1)} %convert_element_type.300), channel_id=1, replica_groups=mesh['dp'=2,'row'=4,'col'=4] {'row'}, dimensions={0}, use_global_device_ids=true | all-gather | bytes 983040 | tf_op jit(solution)/shard_map/all_gather | solution.py:230
  248.5 39.7 %all_gather.102 = bf16[2048,192]{0,1:T(8,128)(2,1)} all-gather(bf16[512,192]{0,1:T(8,128)(2,1)S(1)} %copy-done.60), channel_id=1, replica_groups=mesh['dp'=2,'row'=4,'col'=4] {'row'}, dimensions={0}, use_global_device_ids=true | all-gather | bytes 983040 | tf_op jit(solution)/shard_map/all_gather | solution.py:230
  296.8 17.3 while.57
  314.1 18.3 %all_gather.111 = bf16[2048,192]{0,1:T(8,128)(2,1)S(1)} all-gather(bf16[512,192]{0,1:T(8,128)(2,1)} %bitcast.472), channel_id=1, replica_groups=mesh['dp'=2,'row'=4,'col'=4] {'row'}, dimensions={0}, use_global_device_ids=true | all-gather | bytes 983040 | tf_op jit(solution)/shard_map/all_gather | solution.py:72
  341.1 14.6 while.56
  356.5 17.6 all_gather.103
  384.4 14.9 reduce-scatter.31.cloned.1.call-done
  401.1 12.5 all-reduce.4
  415.5 7.7 all_gather.105
  428.1 108.8 %reduce-scatter.33.cloned.1.call-done = f32[512,768]{1,0:T(8,128)} async-done(((f32[2048,768]{1,0:T(8,128)}), f32[512,768]{1,0:T(8,128)}) %reduce-scatter.33.cloned.1.call-update) | async-done | bytes 1572880 | tf_op jit(solution)/shard_map/reduce_scatter | solution.py:76
  542.5 7.9 all_gather.108
  550.4 56.2 %all-gather.7.cloned.1.call-done = bf16[2048,768]{1,0:T(8,128)(2,1)} async-done(((bf16[512,768]{1,0:T(8,128)(2,1)}), bf16[2048,768]{1,0:T(8,128)(2,1)}) %all-gather.7.cloned.1.call-update) | async-done | bytes 3145744 | tf_op jit(solution)/shard_map/all_gather | solution.py:72
  611.3 21.3 %reduce-scatter.35.cloned.1.call-done = bf16[512,192]{0,1:T(8,128)(2,1)} async-done(((bf16[2048,192]{0,1:T(8,128)(2,1)}), bf16[512,192]{0,1:T(8,128)(2,1)}) %reduce-scatter.35.cloned.1.call-update) | async-done | bytes 196624 | tf_op jit(solution)/shard_map/reduce_scatter | solution.py:80
  635.4 8.2 all_gather.112
  648.3 111.2 %reduce-scatter.41.cloned.1.call-done = f32[512,768]{1,0:T(8,128)} async-done(((f32[2048,768]{1,0:T(8,128)}), f32[512,768]{1,0:T(8,128)}) %reduce-scatter.41.cloned.1.call-update) | async-done | bytes 1572880 | tf_op jit(solution)/shard_map/reduce_scatter | solution.py:76
  765.1 64.1 %all-gather.9.cloned.1.call-done = bf16[2048,768]{1,0:T(8,128)(2,1)} async-done(((bf16[512,768]{1,0:T(8,128)(2,1)}), bf16[2048,768]{1,0:T(8,128)(2,1)}) %all-gather.9.cloned.1.call-update) | async-done | bytes 3145744 | tf_op jit(solution)/shard_map/all_gather | solution.py:72
  834.9 20.3 %reduce-scatter.43.cloned.1.call-done = bf16[512,192]{0,1:T(8,128)(2,1)} async-done(((bf16[2048,192]{0,1:T(8,128)(2,1)}), bf16[512,192]{0,1:T(8,128)(2,1)}) %reduce-scatter.43.cloned.1.call-update) | async-done | bytes 196624 | tf_op jit(solution)/shard_map/reduce_scatter | solution.py:80
  857.9 12.5 all-reduce.3
  874.1 9.2 all-reduce.2
  900.8 8.9 all_gather.114
  915.4 95.9 %reduce-scatter.57.cloned.1.call-done = f32[512,768]{1,0:T(8,128)} async-done(((f32[2048,768]{1,0:T(8,128)}), f32[512,768]{1,0:T(8,128)}) %reduce-scatter.57.cloned.1.call-update) | async-done | bytes 1572880 | tf_op jit(solution)/shard_map/reduce_scatter | solution.py:76
  1015.6 109.1 %reduce-scatter.45.cloned.1.call-done = f32[512,768]{1,0:T(8,128)} async-done(((f32[2048,768]{1,0:T(8,128)}), f32[512,768]{1,0:T(8,128)}) %reduce-scatter.45.cloned.1.call-update) | async-done | bytes 1572880 | tf_op jit(solution)/shard_map/reduce_scatter | solution.py:76
  1128.7 62.2 %all-gather.15.cloned.1.call-done = bf16[2048,768]{1,0:T(8,128)(2,1)} async-done(((bf16[512,768]{1,0:T(8,128)(2,1)}), bf16[2048,768]{1,0:T(8,128)(2,1)}) %all-gather.15.cloned.1.call-update) | async-done | bytes 3145744 | tf_op jit(solution)/shard_map/all_gather | solution.py:72
  1195.0 59.6 %all-gather.11.cloned.1.call-done = bf16[2048,768]{1,0:T(8,128)(2,1)} async-done(((bf16[512,768]{1,0:T(8,128)(2,1)}), bf16[2048,768]{1,0:T(8,128)(2,1)}) %all-gather.11.cloned.1.call-update) | async-done | bytes 3145744 | tf_op jit(solution)/shard_map/all_gather | solution.py:72
  1258.6 20.8 %reduce-scatter.59.cloned.1.call-done = bf16[512,192]{0,1:T(8,128)(2,1)} async-done(((bf16[2048,192]{0,1:T(8,128)(2,1)}), bf16[512,192]{0,1:T(8,128)(2,1)}) %reduce-scatter.59.cloned.1.call-update) | async-done | bytes 196624 | tf_op jit(solution)/shard_map/reduce_scatter | solution.py:80
  1279.4 25.9 %reduce-scatter.47.cloned.1.call-done = bf16[512,192]{0,1:T(8,128)(2,1)} async-done(((bf16[2048,192]{0,1:T(8,128)(2,1)}), bf16[512,192]{0,1:T(8,128)(2,1)}) %reduce-scatter.47.cloned.1.call-update) | async-done | bytes 196624 | tf_op jit(solution)/shard_map/reduce_scatter | solution.py:80
  1308.9 12.5 all-reduce.1
  1337.6 29.0 %all_gather.117 = bf16[2048,192]{0,1:T(8,128)(2,1)} all-gather(bf16[512,192]{0,1:T(8,128)(2,1)S(1)} %slice.241), channel_id=1, replica_groups=mesh['dp'=2,'row'=4,'col'=4] {'row'}, dimensions={0}, use_global_device_ids=true | all-gather | bytes 983040 | tf_op jit(solution)/shard_map/all_gather | solution.py:281
  1370.1 23.5 %all_gather.122 = bf16[2048,192]{0,1:T(8,128)(2,1)} all-gather(bf16[512,192]{0,1:T(8,128)(2,1)S(1)} %slice.240), channel_id=1, replica_groups=mesh['dp'=2,'row'=4,'col'=4] {'row'}, dimensions={0}, use_global_device_ids=true | all-gather | bytes 983040 | tf_op jit(solution)/shard_map/all_gather | solution.py:281
  1396.0 8.8 all_gather.116
  1414.5 30.3 %while.59 = (s32[]{:T(128)}, f32[3,512,64]{1,2,0:T(8,128)}, bf16[3,2048,64]{1,2,0:T(8,128)(2,1)}, bf16[3,2048,64]{1,2,0:T(8,128)(2,1)}, bf16[3,512,64]{2,1,0:T(8...) while((s32[]{:T(128)}, f32[3,512,64]{1,2,0:T(8,128)}, ...), condition=%wide.region_62.63_spmd.clone, body=%wide.region_60.62_spmd.clone.sunk | while | flops 680691200 | bytes 48123144 | solution.py:166
  1448.2 24.9 %while.58 = (s32[]{:T(128)}, f32[3,512,64]{1,2,0:T(8,128)}, bf16[3,2048,64]{1,2,0:T(8,128)(2,1)}, bf16[3,2048,64]{1,2,0:T(8,128)(2,1)S(1)}, bf16[3,512,64]{2,1,0...) while((s32[]{:T(128)}, f32[3,512,64]{1,2,0:T(8,128)}, ...), condition=%wide.region_45.46_spmd.clone, body=%wide.region_43.45_spmd.clone.sunk | while | flops 680691200 | bytes 41045172 | solution.py:166
  1476.5 19.5 %reduce-scatter.51.cloned.1.call-done = bf16[512,192]{0,1:T(8,128)(2,1)} async-done(((bf16[2048,192]{0,1:T(8,128)(2,1)}), bf16[512,192]{0,1:T(8,128)(2,1)}) %reduce-scatter.51.cloned.1.call-update) | async-done | bytes 196624 | tf_op jit(solution)/shard_map/reduce_scatter | solution.py:293
  1501.4 19.5 %reduce-scatter.53.cloned.1.call-done = bf16[512,192]{0,1:T(8,128)(2,1)} async-done(((bf16[2048,192]{0,1:T(8,128)(2,1)}), bf16[512,192]{0,1:T(8,128)(2,1)}) %reduce-scatter.53.cloned.1.call-update) | async-done | bytes 196624 | tf_op jit(solution)/shard_map/reduce_scatter | solution.py:299
  1523.8 21.9 %reduce-scatter.65.cloned.1.call-done = bf16[512,192]{0,1:T(8,128)(2,1)} async-done(((bf16[2048,192]{0,1:T(8,128)(2,1)}), bf16[512,192]{0,1:T(8,128)(2,1)}) %reduce-scatter.65.cloned.1.call-update) | async-done | bytes 196624 | tf_op jit(solution)/shard_map/reduce_scatter | solution.py:299
  1560.2 37.4 %all-gather.13.cloned.1.call-done = bf16[2048,576]{0,1:T(8,128)(2,1)} async-done(((bf16[512,576]{0,1:T(8,128)(2,1)}), bf16[2048,576]{0,1:T(8,128)(2,1)}) %all-gather.13.cloned.1.call-update) | async-done | bytes 2359312 | tf_op jit(solution)/shard_map/all_gather | solution.py:72
  1600.4 48.1 %all-gather.17.cloned.1.call-done = bf16[2048,576]{0,1:T(8,128)(2,1)} async-done(((bf16[512,576]{0,1:T(8,128)(2,1)}), bf16[2048,576]{0,1:T(8,128)(2,1)}) %all-gather.17.cloned.1.call-update) | async-done | bytes 2359312 | tf_op jit(solution)/shard_map/all_gather | solution.py:72
  1664.5 13.0 reduce-scatter.77.cloned.1.call-done
  1679.2 13.3 all-reduce
  1694.0 8.6 reduce-scatter.69.cloned.1.call-done
  1704.0 10.9 reduce-scatter.71.cloned.1.call-done
  1716.3 10.7 reduce-scatter.73.cloned.1.call-done
  1728.5 25.1 %reduce-scatter.55.cloned.1.call-done = bf16[512,192]{0,1:T(8,128)(2,1)} async-done(((bf16[2048,192]{0,1:T(8,128)(2,1)}), bf16[512,192]{0,1:T(8,128)(2,1)}) %reduce-scatter.55.cloned.1.call-update) | async-done | bytes 196624 | tf_op jit(solution)/shard_map/reduce_scatter | solution.py:80
  1753.6 25.9 %reduce-scatter.67.cloned.1.call-done = bf16[512,192]{0,1:T(8,128)(2,1)} async-done(((bf16[2048,192]{0,1:T(8,128)(2,1)}), bf16[512,192]{0,1:T(8,128)(2,1)}) %reduce-scatter.67.cloned.1.call-update) | async-done | bytes 196624 | tf_op jit(solution)/shard_map/reduce_scatter | solution.py:80
  (526 shorter events, 345.6 us)
Async XLA Ops:
  7.2 115.0 %reduce-scatter.29.cloned.1.call-start = ((), (), s32[]{:S(2)}) async-start(), calls=%async_computation.26 | async-start | bytes 5898240 | tf_op jit(solution)/shard_map/reduce_scatter | solution.py:76
  36.4 173.9 %reduce-scatter.37.cloned.1.call-start = ((), (), s32[]{:S(2)}) async-start(), calls=%async_computation.31 | async-start | bytes 5898240 | tf_op jit(solution)/shard_map/reduce_scatter | solution.py:76
  48.4 336.0 %reduce-scatter.39.cloned.1.call-start = ((), (), s32[]{:S(2)}) async-start(), calls=%async_computation.32 | async-start | bytes 983040 | tf_op jit(solution)/shard_map/reduce_scatter | solution.py:80
  48.5 169.0 %copy-start.49 = (bf16[3,512,64]{1,2,0:T(8,128)(2,1)}, bf16[3,512,64]{1,2,0:T(8,128)(2,1)S(1)}, u32[]{:S(2)}) copy-start(bf16[3,512,64]{1,2,0:T(8,128)(2,1)S(1)} %fusion.145) | copy-start | bytes 589828
  56.2 158.9 %copy-start.61 = (f32[512,32]{0,1:T(8,128)}, f32[512,32]{0,1:T(8,128)S(1)}, u32[]{:S(2)}) copy-start(f32[512,32]{0,1:T(8,128)S(1)} %get-tuple-element.549) | copy-start | bytes 196612
  123.9 114.5 %collective-permute-start = (bf16[1,512,192]{1,2,0:T(8,128)(2,1)}, bf16[1,512,192]{1,2,0:T(8,128)(2,1)}, u32[]{:S(2)}, u32[]{:S(2)}) collective-permute-start(bf16[1,512,192]{1,2,0:T(8,128)(2,1)} %slice_bitcast_fusion.2), channel_id=1, source_target_pairs={{0,4},{4,0},{8,12},{12,8},{1,5},{5,1},{9,13},{13,9},{2,6},{6,2},{1... | collective-permute-start | bytes 589832 | tf_op jit(solution)/shard_map/ppermute | solution.py:22
  212.0 29.3 %collective-permute-start.2 = (bf16[1,512,192]{1,2,0:T(8,128)(2,1)}, bf16[1,512,192]{1,2,0:T(8,128)(2,1)}, u32[]{:S(2)}, u32[]{:S(2)}) collective-permute-start(bf16[1,512,192]{1,2,0:T(8,128)(2,1)} %slice_bitcast_fusion.3), channel_id=1, source_target_pairs={{0,4},{4,0},{8,12},{12,8},{1,5},{5,1},{9,13},{13,9},{2,6},{6,2},{1... | collective-permute-start | bytes 589832 | tf_op jit(solution)/shard_map/ppermute | solution.py:22
  240.4 49.5 %collective-permute-start.1 = (bf16[2,512,192]{1,2,0:T(8,128)(2,1)}, bf16[2,512,192]{1,2,0:T(8,128)(2,1)}, u32[]{:S(2)}, u32[]{:S(2)}) collective-permute-start(bf16[2,512,192]{1,2,0:T(8,128)(2,1)} %pad_maximum_fusion.5), channel_id=1, source_target_pairs={{0,8},{4,12},{8,0},{12,4},{1,9},{5,13},{9,1},{13,5},{2,10},{6,14},... | collective-permute-start | bytes 1179656 | tf_op jit(solution)/shard_map/ppermute | solution.py:22
  243.3 46.7 %collective-permute-start.3 = (bf16[2,512,192]{1,2,0:T(8,128)(2,1)}, bf16[2,512,192]{1,2,0:T(8,128)(2,1)}, u32[]{:S(2)}, u32[]{:S(2)}) collective-permute-start(bf16[2,512,192]{1,2,0:T(8,128)(2,1)} %pad_maximum_fusion.6), channel_id=1, source_target_pairs={{0,8},{4,12},{8,0},{12,4},{1,9},{5,13},{9,1},{13,5},{2,10},{6,14},... | collective-permute-start | bytes 1179656 | tf_op jit(solution)/shard_map/ppermute | solution.py:22
  335.5 63.8 %reduce-scatter.31.cloned.1.call-start = ((), (), s32[]{:S(2)}) async-start(), calls=%async_computation.27 | async-start | bytes 983040 | tf_op jit(solution)/shard_map/reduce_scatter | solution.py:80
  377.2 159.6 %reduce-scatter.33.cloned.1.call-start = ((), (), s32[]{:S(2)}) async-start(), calls=%async_computation.28 | async-start | bytes 7864320 | tf_op jit(solution)/shard_map/reduce_scatter | solution.py:76
  427.8 178.8 %all-gather.7.cloned.1.call-start = ((), (), s32[]{:S(2)}) async-start(), calls=%async_computation.29 | async-start | bytes 3932160 | tf_op jit(solution)/shard_map/all_gather | solution.py:72
  542.4 90.2 %reduce-scatter.35.cloned.1.call-start = ((), (), s32[]{:S(2)}) async-start(), calls=%async_computation.30 | async-start | bytes 983040 | tf_op jit(solution)/shard_map/reduce_scatter | solution.py:80
  610.5 149.0 %reduce-scatter.41.cloned.1.call-start = ((), (), s32[]{:S(2)}) async-start(), calls=%async_computation.33 | async-start | bytes 7864320 | tf_op jit(solution)/shard_map/reduce_scatter | solution.py:76
  648.2 181.0 %all-gather.9.cloned.1.call-start = ((), (), s32[]{:S(2)}) async-start(), calls=%async_computation.34 | async-start | bytes 3932160 | tf_op jit(solution)/shard_map/all_gather | solution.py:72
  765.0 90.2 %reduce-scatter.43.cloned.1.call-start = ((), (), s32[]{:S(2)}) async-start(), calls=%async_computation.35 | async-start | bytes 983040 | tf_op jit(solution)/shard_map/reduce_scatter | solution.py:80
  833.2 178.1 %reduce-scatter.57.cloned.1.call-start = ((), (), s32[]{:S(2)}) async-start(), calls=%async_computation.44 | async-start | bytes 7864320 | tf_op jit(solution)/shard_map/reduce_scatter | solution.py:76
  900.8 224.0 %reduce-scatter.45.cloned.1.call-start = ((), (), s32[]{:S(2)}) async-start(), calls=%async_computation.36 | async-start | bytes 7864320 | tf_op jit(solution)/shard_map/reduce_scatter | solution.py:76
  915.4 275.6 %all-gather.15.cloned.1.call-start = ((), (), s32[]{:S(2)}) async-start(), calls=%async_computation.45 | async-start | bytes 3932160 | tf_op jit(solution)/shard_map/all_gather | solution.py:72
  1015.2 239.4 %all-gather.11.cloned.1.call-start = ((), (), s32[]{:S(2)}) async-start(), calls=%async_computation.37 | async-start | bytes 3932160 | tf_op jit(solution)/shard_map/all_gather | solution.py:72
  1128.6 150.8 %reduce-scatter.59.cloned.1.call-start = ((), (), s32[]{:S(2)}) async-start(), calls=%async_computation.46 | async-start | bytes 983040 | tf_op jit(solution)/shard_map/reduce_scatter | solution.py:80
  1194.9 110.3 %reduce-scatter.47.cloned.1.call-start = ((), (), s32[]{:S(2)}) async-start(), calls=%async_computation.38 | async-start | bytes 983040 | tf_op jit(solution)/shard_map/reduce_scatter | solution.py:80
  1258.5 149.7 %reduce-scatter.61.cloned.1.call-start = ((), (), s32[]{:S(2)}) async-start(), calls=%async_computation.47 | async-start | bytes 1966080 | tf_op jit(solution)/shard_map/reduce_scatter | solution.py:76
  1336.5 108.5 %reduce-scatter.49.cloned.1.call-start = ((), (), s32[]{:S(2)}) async-start(), calls=%async_computation.39 | async-start | bytes 1966080 | tf_op jit(solution)/shard_map/reduce_scatter | solution.py:76
  1408.1 67.2 %reduce-scatter.63.cloned.1.call-start = ((), (), s32[]{:S(2)}) async-start(), calls=%async_computation.48 | async-start | bytes 983040 | tf_op jit(solution)/shard_map/reduce_scatter | solution.py:293
  1444.9 51.2 %reduce-scatter.51.cloned.1.call-start = ((), (), s32[]{:S(2)}) async-start(), calls=%async_computation.40 | async-start | bytes 983040 | tf_op jit(solution)/shard_map/reduce_scatter | solution.py:293
  1473.1 47.7 %reduce-scatter.53.cloned.1.call-start = ((), (), s32[]{:S(2)}) async-start(), calls=%async_computation.41 | async-start | bytes 983040 | tf_op jit(solution)/shard_map/reduce_scatter | solution.py:299
  1474.0 71.7 %reduce-scatter.65.cloned.1.call-start = ((), (), s32[]{:S(2)}) async-start(), calls=%async_computation.49 | async-start | bytes 983040 | tf_op jit(solution)/shard_map/reduce_scatter | solution.py:299
  1474.8 122.9 %all-gather.13.cloned.1.call-start = ((), (), s32[]{:S(2)}) async-start(), calls=%async_computation.42 | async-start | bytes 2949120 | tf_op jit(solution)/shard_map/all_gather | solution.py:72
  1522.7 125.8 %all-gather.17.cloned.1.call-start = ((), (), s32[]{:S(2)}) async-start(), calls=%async_computation.50 | async-start | bytes 2949120 | tf_op jit(solution)/shard_map/all_gather | solution.py:72
  1547.6 115.1 %reduce-scatter.79.cloned.1.call-start = ((), (), s32[]{:S(2)}) async-start(), calls=%async_computation.57 | async-start | bytes 589824
  1552.5 125.1 %reduce-scatter.77.cloned.1.call-start = ((), (), s32[]{:S(2)}) async-start(), calls=%async_computation.56 | async-start | bytes 442368 | tf_op jit(solution)/shard_map/reduce_scatter | solution.py:330
  1557.6 135.0 %reduce-scatter.75.cloned.1.call-start = ((), (), s32[]{:S(2)}) async-start(), calls=%async_computation.55 | async-start | bytes 147456 | tf_op jit(solution)/shard_map/reduce_scatter | solution.py:327
  1560.0 88.5 %copy-start.30 = (bf16[2048,192]{0,1:T(8,128)(2,1)S(1)}, bf16[2048,192]{0,1:T(8,128)(2,1)}, u32[]{:S(2)}) copy-start(bf16[2048,192]{0,1:T(8,128)(2,1)} %copy-done.29) | copy-start | bytes 2359300
  1560.0 142.6 %reduce-scatter.69.cloned.1.call-start = ((), (), s32[]{:S(2)}) async-start(), calls=%async_computation.52 | async-start | bytes 147456 | tf_op jit(solution)/shard_map/reduce_scatter | solution.py:315
  1652.0 62.9 %reduce-scatter.71.cloned.1.call-start = ((), (), s32[]{:S(2)}) async-start(), calls=%async_computation.53 | async-start | bytes 147456 | tf_op jit(solution)/shard_map/reduce_scatter | solution.py:318
  1652.8 74.3 %reduce-scatter.73.cloned.1.call-start = ((), (), s32[]{:S(2)}) async-start(), calls=%async_computation.54 | async-start | bytes 147456 | tf_op jit(solution)/shard_map/reduce_scatter | solution.py:324
  1653.4 100.3 %reduce-scatter.55.cloned.1.call-start = ((), (), s32[]{:S(2)}) async-start(), calls=%async_computation.43 | async-start | bytes 983040 | tf_op jit(solution)/shard_map/reduce_scatter | solution.py:80
  1657.0 122.5 %reduce-scatter.67.cloned.1.call-start = ((), (), s32[]{:S(2)}) async-start(), calls=%async_computation.51 | async-start | bytes 983040 | tf_op jit(solution)/shard_map/reduce_scatter | solution.py:80
  1658.8 120.7 %copy-start.20 = (bf16[512,192]{0,1:T(8,128)(2,1)S(1)}, bf16[512,192]{0,1:T(8,128)(2,1)}, u32[]{:S(2)}) copy-start(bf16[512,192]{0,1:T(8,128)(2,1)} %reduce-scatter.31.cloned.1.call-done) | copy-start | bytes 589828
  1658.8 120.7 %copy-start.21 = (bf16[512,192]{0,1:T(8,128)(2,1)S(1)}, bf16[512,192]{0,1:T(8,128)(2,1)}, u32[]{:S(2)}) copy-start(bf16[512,192]{0,1:T(8,128)(2,1)} %reduce-scatter.39.cloned.1.call-done) | copy-start | bytes 589828
  1658.8 120.6 %copy-start.23 = (f32[512,192]{0,1:T(8,128)S(1)}, f32[512,192]{0,1:T(8,128)}, u32[]{:S(2)}) copy-start(f32[512,192]{0,1:T(8,128)} %get-tuple-element.473) | copy-start | bytes 1179652
  1658.8 120.6 %copy-start.24 = (f32[512,192]{0,1:T(8,128)S(1)}, f32[512,192]{0,1:T(8,128)}, u32[]{:S(2)}) copy-start(f32[512,192]{0,1:T(8,128)} %get-tuple-element.474) | copy-start | bytes 1179652
  1658.9 120.6 %copy-start.66 = (f32[192]{0:T(256)S(1)}, f32[192]{0:T(256)}, u32[]{:S(2)}) copy-start(f32[192]{0:T(256)} %param.28) | copy-start | bytes 2308
  1658.9 120.6 %copy-start.72 = (f32[512]{0:T(512)S(1)}, f32[512]{0:T(512)}, u32[]{:S(2)}) copy-start(f32[512]{0:T(512)} %copy-done.71) | copy-start | bytes 6148
  1658.9 120.6 %copy-start.74 = (f32[512]{0:T(512)S(1)}, f32[512]{0:T(512)}, u32[]{:S(2)}) copy-start(f32[512]{0:T(512)} %copy-done.73) | copy-start | bytes 6148
  1658.9 120.6 %copy-start.76 = (f32[512]{0:T(512)S(1)}, f32[512]{0:T(512)}, u32[]{:S(2)}) copy-start(f32[512]{0:T(512)} %copy-done.75) | copy-start | bytes 6148
  1658.9 120.6 %copy-start.78 = (f32[512]{0:T(512)S(1)}, f32[512]{0:T(512)}, u32[]{:S(2)}) copy-start(f32[512]{0:T(512)} %copy-done.77) | copy-start | bytes 6148
  (98 other events, 721.0 us)
Sparse Core Ops, SparseCore 0:
  36.6 85.5 reduce-scatter.28
  124.5 85.7 reduce-scatter.36
  335.6 22.5 reduce-scatter.38
  377.3 21.9 reduce-scatter.30
  427.9 108.9 reduce-scatter.32
  542.5 63.9 all-gather.6
  610.7 21.8 reduce-scatter.34
  648.3 111.1 reduce-scatter.40
  765.1 64.0 all-gather.8
  833.3 21.9 reduce-scatter.42
  900.9 110.3 reduce-scatter.56
  1013.4 111.2 reduce-scatter.44
  1126.9 64.0 all-gather.14
  1192.4 62.1 all-gather.10
  1257.5 21.8 reduce-scatter.58
  1282.0 23.2 reduce-scatter.46
  1336.7 50.1 reduce-scatter.60
  1408.2 34.7 reduce-scatter.48
  1445.3 22.3 reduce-scatter.62
  1473.3 22.6 reduce-scatter.50
  1498.3 22.5 reduce-scatter.52
  1523.2 22.5 reduce-scatter.64
  1547.9 49.6 all-gather.12
  1599.1 49.3 all-gather.16
  1650.7 11.9 reduce-scatter.78
  1665.5 12.0 reduce-scatter.76
  1679.7 9.9 reduce-scatter.74
  1692.6 9.9 reduce-scatter.68
  1704.9 9.9 reduce-scatter.70
  1717.0 9.9 reduce-scatter.72
  1730.3 23.2 reduce-scatter.54
  1756.2 23.2 reduce-scatter.66
